TPU v7x, 512 devices: a whole 4x4x16 slice. The times are simulated.
512 devices in a mesh: batch: 32 (over x, z_lo), tensor: 16 (over y, z_hi, core).
Axes of the slice: x: 4, y: 4, z: 16 (z_hi: 2, z_lo: 8; z = z_hi * 8 + z_lo), core: 2. Of those that a mesh axis runs over, the one named last changes fastest.
Arguments:
- hidden_in: bfloat16 [16384, 8192], P('batch', 'tensor'), may hold values from -1600 to 1600, as said below
- norm_gain: bfloat16 [8192], P('tensor'), may hold values from 0.099609375 to 1.8984375
- q_weight: bfloat16 [8192, 4096], P(('batch', 'tensor')), may hold values from -0.4087961 to 0.4087961, as said below
- k_weight: bfloat16 [8192, 512], P(('batch', 'tensor')), may hold values from -0.044194174 to 0.044194174, as said below
- v_weight: bfloat16 [8192, 512], P(('batch', 'tensor')), may hold values from -0.0625 to 0.0625
Outputs:
- head_out: bfloat16 [16384, 4096], P('batch', 'tensor')
Inputs may be any that keep to these rules, and one draw needn't show every extreme that they name: `hidden_in`: activations with independent scales over rows and over features. `q_weight`: A dense matrix. `k_weight`: A dense matrix.
All inputs are finite; a program needn't handle non-finite values.
Results may differ from a plain program's by a relative error of at most 0.008.
Values may be sent and summed in bfloat16 or wider, within the bound.
A program may use at most 128 MiB of HBM per device.

v0:
```python
import jax
import jax.numpy as jnp
from jax import lax
from jax.sharding import PartitionSpec as P

HD = 128


def rotate_heads(field, head_size):
    seq_len = field.shape[0]
    heads = field.shape[1] // head_size
    shaped = field.reshape(seq_len, heads, head_size)
    half = head_size // 2
    position = jnp.arange(seq_len, dtype=jnp.float32)
    freqs = 500000.0 ** (-(jnp.arange(half, dtype=jnp.float32) * 2.0) / head_size)
    angles = position[:, None] * freqs[None, :]
    cosine = jnp.cos(angles)[:, None, :]
    sine = jnp.sin(angles)[:, None, :]
    first = shaped[..., :half]
    second = shaped[..., half:]
    turned = jnp.concatenate(
        [first * cosine - second * sine, second * cosine + first * sine], axis=-1
    )
    return turned.astype(jnp.bfloat16)


def on_device(hidden_in, norm_gain, q_weight, k_weight, v_weight):
    tensor_count = lax.axis_size("tensor")
    whole_rows, whole_gain = (
        lax.all_gather(hidden_in, "tensor", axis=1, tiled=True),
        lax.all_gather(norm_gain, "tensor", axis=0, tiled=True),
    )
    values = whole_rows.astype(jnp.float32)
    meansq = jnp.mean(values * values, axis=-1, keepdims=True)
    normed = (values * lax.rsqrt(meansq + 1e-05) * whole_gain.astype(jnp.float32)).astype(
        jnp.bfloat16
    )
    own_rows = q_weight.shape[0]
    kv_heads = k_weight.shape[1] // HD
    repeat_count = tensor_count // kv_heads
    q_send = q_weight.reshape(own_rows, tensor_count, -1)
    k_send = jnp.repeat(k_weight.reshape(own_rows, kv_heads, HD), repeat_count, axis=1)
    v_send = jnp.repeat(v_weight.reshape(own_rows, kv_heads, HD), repeat_count, axis=1)
    q_recv, k_recv, v_recv = (
        lax.all_to_all(q_send, "tensor", split_axis=1, concat_axis=0, tiled=True),
        lax.all_to_all(k_send, "tensor", split_axis=1, concat_axis=0, tiled=True),
        lax.all_to_all(v_send, "tensor", split_axis=1, concat_axis=0, tiled=True),
    )
    q_block = q_recv.reshape(q_recv.shape[0], q_recv.shape[2])
    k_block = k_recv.reshape(k_recv.shape[0], k_recv.shape[2])
    v_block = v_recv.reshape(v_recv.shape[0], v_recv.shape[2])
    seq_len = normed.shape[0]
    q_full, k_full, v_full = (
        lax.all_gather(q_block, "batch", axis=0, tiled=True),
        lax.all_gather(k_block, "batch", axis=0, tiled=True),
        lax.all_gather(v_block, "batch", axis=0, tiled=True),
    )
    q_lin = jnp.dot(normed, q_full, preferred_element_type=jnp.float32)
    k_lin = jnp.dot(normed, k_full, preferred_element_type=jnp.float32)
    v_lin = jnp.dot(normed, v_full, preferred_element_type=jnp.float32)
    q_rot = rotate_heads(q_lin, HD)
    k_rot = rotate_heads(k_lin, HD)[:, 0, :]
    v_val = v_lin.astype(jnp.bfloat16)
    scores = jnp.einsum("shd,td->hst", q_rot, k_rot, preferred_element_type=jnp.float32) / jnp.sqrt(
        jnp.float32(HD)
    )
    causal = jnp.tril(jnp.ones((seq_len, seq_len), dtype=bool))
    scores = jnp.where(causal[None], scores, jnp.float32(-1e30))
    top = jnp.max(scores, axis=-1, keepdims=True)
    expo = jnp.exp(scores - top)
    probs = (expo / jnp.sum(expo, axis=-1, keepdims=True)).astype(jnp.bfloat16)
    result = jnp.einsum("hst,td->shd", probs, v_val, preferred_element_type=jnp.float32)
    return result.astype(jnp.bfloat16).reshape(seq_len, -1)


def solution(mesh):
    placed = (
        P("batch", "tensor"),
        P("tensor"),
        P(("batch", "tensor"), None),
        P(("batch", "tensor"), None),
        P(("batch", "tensor"), None),
    )
    return jax.shard_map(
        on_device, mesh=mesh, in_specs=placed, out_specs=P("batch", "tensor"), check_vma=False
    )
```

profile of v0, /device:TPU:24, one launch (start us, length us, event | category | flops | bytes accessed | tf_op | source)
XLA Modules:
  0.0 904.1 jit_solution(9239658966304394324)
XLA Ops:
  6.5 0.7 all-gather.6.cloned.1.call-update
  7.3 0.0 all-gather.12.cloned.1.call-start
  7.3 0.9 copy.49
  8.2 31.0 %all_to_all.45 = bf16[16,16,256]{2,0,1:T(8,128)(2,1)} all-to-all(bf16[16,16,256]{2,0,1:T(8,128)(2,1)S(1)} %bitcast.70), channel_id=1, replica_groups=mesh['batch'=32,'tensor'=16] {'tensor'}, dimensions={1} | all-to-all | bytes 262144 | tf_op jit(solution)/shard_map/all_to_all | solution.py:45
  39.2 0.0 all-gather.12.cloned.1.call-update
  39.3 0.0 all-gather.10.cloned.1.call-start
  39.4 19.9 %all_to_all.46 = bf16[16,16,128]{2,0,1:T(8,128)(2,1)} all-to-all(bf16[16,16,128]{2,0,1:T(8,128)(2,1)S(1)} %bitcast.71), channel_id=1, replica_groups=mesh['batch'=32,'tensor'=16] {'tensor'}, dimensions={1} | all-to-all | bytes 131072 | tf_op jit(solution)/shard_map/all_to_all | solution.py:46
  59.3 0.0 all-gather.10.cloned.1.call-update
  59.3 0.7 copy_bitcast_fusion.2
  60.0 0.6 broadcast_in_dim.13
  60.7 12.5 %all-to-all-start = ((bf16[16,16,128]{2,0,1:T(8,128)(2,1)}), bf16[16,16,128]{2,0,1:T(8,128)(2,1)S(1)}, u32[]{:S(2)}, u32[]{:S(2)}) async-start(bf16[16,16,128]{2,0,1:T(8,128)(2,1)} %bitcast.1), calls=%async_computation | async-start | bytes 131072 | tf_op jit(solution)/shard_map/all_to_all | solution.py:47
  73.2 0.0 all-gather.8.cloned.1.call-start
  73.2 0.1 iota_compare_fusion
  73.3 0.7 reshape.147
  74.0 54.4 %all-gather = bf16[16,1,512]{2,1,0:T(2,128)(2,1)S(1)} all-gather(bf16[1,1,512]{2,1,0:T(2,128)(2,1)S(1)} %reshape.147), channel_id=1, replica_groups=mesh['batch'=32,'tensor'=16] {'tensor'}, dimensions={0}, use_global_device_ids=true | all-gather | bytes 17408 | tf_op jit(solution)/shard_map/all_gather | solution.py:31
  128.4 1.0 fusion.14
  129.4 0.6 copy-done.1
  130.1 72.7 %all-gather.6.cloned.1.call-done = bf16[512,8192]{1,0:T(8,128)(2,1)} async-done(((bf16[512,512]{1,0:T(8,128)(2,1)}), bf16[512,8192]{1,0:T(8,128)(2,1)}) %all-gather.6.cloned.1.call-update) | async-done | bytes 8388624 | tf_op jit(solution)/shard_map/all_gather | solution.py:30
  202.8 5.1 fusion.1
  207.9 9.8 %fusion.3 = bf16[512,8192]{1,0:T(8,128)(2,1)} fusion(bf16[512,8192]{1,0:T(8,128)(2,1)} %all-gather.6.cloned.1.call-done, f32[8192]{0:T(1024)S(1)} %bitcast.75, f32[512]{0:T(512)S(1)} %add_rsqrt_fusion), kind=kLoop, calls=%fused_computation.5 | loop fusion | flops 16777216 | bytes 16812032 | tf_op jit(solution)/shard_map/convert_element_type | solution.py:35
  217.8 216.6 %all-gather.12.cloned.1.call-done = bf16[8192,256]{1,0:T(8,128)(2,1)} async-done(((bf16[256,256]{1,0:T(8,128)(2,1)}), bf16[8192,256]{1,0:T(8,128)(2,1)}) %all-gather.12.cloned.1.call-update) | async-done | bytes 4194320 | tf_op jit(solution)/shard_map/all_gather | solution.py:54
  434.4 6.9 fusion.34
  441.4 0.2 copy.41
  441.6 0.2 copy.42
  441.8 220.7 %all-gather.10.cloned.1.call-done = bf16[8192,128]{1,0:T(8,128)(2,1)} async-done(((bf16[256,128]{1,0:T(8,128)(2,1)}), bf16[8192,128]{1,0:T(8,128)(2,1)}) %all-gather.10.cloned.1.call-update) | async-done | bytes 2097168 | tf_op jit(solution)/shard_map/all_gather | solution.py:55
  662.5 6.9 convolution_bitcast_fusion
  669.4 0.6 fusion.23
  669.9 0.1 subtract_convert_fusion
  670.1 2.5 fusion.31
  672.6 216.6 %all-gather.8.cloned.1.call-done = bf16[8192,128]{1,0:T(8,128)(2,1)} async-done(((bf16[256,128]{1,0:T(8,128)(2,1)}), bf16[8192,128]{1,0:T(8,128)(2,1)}) %all-gather.8.cloned.1.call-update) | async-done | bytes 2097168 | tf_op jit(solution)/shard_map/all_gather | solution.py:56
  889.3 7.4 convolution_convert_fusion
  896.7 0.8 copy.35
  (12 shorter events, 0.1 us)
Async XLA Ops:
  6.5 32.8 %copy-start = (bf16[16,512]{1,0:T(8,128)(2,1)S(1)}, bf16[16,512]{1,0:T(8,128)(2,1)}, u32[]{:S(2)}) copy-start(bf16[16,512]{1,0:T(8,128)(2,1)} %param.8) | copy-start | bytes 49156
  6.5 196.3 %all-gather.6.cloned.1.call-start = ((), (), s32[]{:S(2)}) async-start(), calls=%async_computation.3 | async-start | bytes 8912896 | tf_op jit(solution)/shard_map/all_gather | solution.py:30
  7.3 427.1 %all-gather.12.cloned.1.call-start = ((), (), s32[]{:S(2)}) async-start(), calls=%async_computation.6 | async-start | bytes 4325376 | tf_op jit(solution)/shard_map/all_gather | solution.py:54
  39.3 623.2 %all-gather.10.cloned.1.call-start = ((), (), s32[]{:S(2)}) async-start(), calls=%async_computation.5 | async-start | bytes 2162688 | tf_op jit(solution)/shard_map/all_gather | solution.py:55
  60.7 68.7 %all-to-all-start = ((bf16[16,16,128]{2,0,1:T(8,128)(2,1)}), bf16[16,16,128]{2,0,1:T(8,128)(2,1)S(1)}, u32[]{:S(2)}, u32[]{:S(2)}) async-start(bf16[16,16,128]{2,0,1:T(8,128)(2,1)} %bitcast.1), calls=%async_computation | async-start | bytes 131072 | tf_op jit(solution)/shard_map/all_to_all | solution.py:47
  73.2 816.1 %all-gather.8.cloned.1.call-start = ((), (), s32[]{:S(2)}) async-start(), calls=%async_computation.4 | async-start | bytes 2162688 | tf_op jit(solution)/shard_map/all_gather | solution.py:56
  129.4 0.6 copy-start.1
Sparse Core Ops, SparseCore 0:
  10.5 192.2 all-gather.5
  204.9 229.4 all-gather.11
  436.5 225.9 all-gather.9
  664.4 224.7 all-gather.7
where the time goes:
time: 905 us; the launch traced here: 904 us
  waiting for transfers between devices  727 us (80%)
  blocking collectives  105 us (12%)
  matrix products  23.8 us (3%)
  other arithmetic  16.8 us (2%)
  between operations  13.3 us (1%)
  starting transfers between devices  12.6 us (1%)
    all_gather x1, waiting for transfers between devices, on_device(): lax.all_gather(k_block, 'batch', axis=0, tiled=True)  221 us
    all_gather x1, waiting for transfers between devices, on_device(): lax.all_gather(v_block, 'batch', axis=0, tiled=True)  217 us
    all_gather x1, waiting for transfers between devices, on_device(): lax.all_gather(q_block, 'batch', axis=0, tiled=True)  217 us
    all_gather x1, waiting for transfers between devices, on_device(): lax.all_gather(hidden_in, 'tensor', axis=1, tiled=True)  72.7 us
    all_gather x1, blocking collectives, on_device(): lax.all_gather(norm_gain, 'tensor', axis=0, tiled=True)  54.4 us
    all_to_all x1, blocking collectives, on_device(): lax.all_to_all(q_send, 'tensor', split_axis=1, concat_axis=0, tiled=True)  31 us
    all_to_all x1, blocking collectives, on_device(): lax.all_to_all(k_send, 'tensor', split_axis=1, concat_axis=0, tiled=True)  19.9 us
  transfers between devices with their start and end apart: 5, of which 4 were waited for; matrix products, arithmetic and copies ran while one was open for 4% of the time, Pallas kernels for 0%

commit v1 on v0

v1 whole, which is shorter than its diff:
```python
import functools

import jax
import jax.numpy as jnp
import numpy as np
from jax import lax
from jax.experimental import pallas as pl
from jax.experimental.pallas import tpu as pltpu
from jax.sharding import PartitionSpec as P

MESH = pl.DeviceIdType.MESH
BF16 = jnp.bfloat16
F32 = jnp.float32
HD = 128
SEQ = 512
ROWS = 128
CHUNKS = SEQ // ROWS
BLK = 512
D = 8192
SCALE = 1.0 / float(np.sqrt(np.float32(HD)))


def tables():
    position = np.arange(SEQ, dtype=np.float32)
    half = HD // 2
    freqs = np.power(np.float32(500000.0), -(np.arange(half, dtype=np.float32) * np.float32(2.0)) / np.float32(HD))
    angles = (position[:, None] * freqs[None, :].astype(np.float32)).astype(np.float32).astype(np.float64)
    cosine = np.cos(angles).astype(np.float32)
    sine = np.sin(angles).astype(np.float32)
    return np.concatenate([cosine, cosine], axis=1), np.concatenate([-sine, sine], axis=1)


def remote(src, dst, send, recv, device):
    return pltpu.make_async_remote_copy(
        src_ref=src, dst_ref=dst, send_sem=send, recv_sem=recv, device_id=device, device_id_type=MESH
    )


def kernel(
    hid, gain, qw, kw, vw, cos, sin, out,
    Z, W, H, R, S1, S2, PO, SB, RB, KB, VB,
    zr, zs, xr, xs, w1s, s1r, s1s, s2r, s2s, rr, rs, opr, ops, hr, hs_, hfr, hfs, er, es,
):
    b = lax.axis_index("batch")
    t = lax.axis_index("tensor")
    x, l = b // 8, b % 8
    y, h, c = t // 4, (t // 2) % 2, t % 2
    z = 8 * h + l
    oc = 1 - c

    def dev(xx, yy, zz, cc):
        return (8 * xx + zz % 8, 4 * yy + 2 * (zz // 8) + cc)

    xp, xm = (x + 1) % 4, (x + 3) % 4
    yp, ym, yo = (y + 1) % 4, (y + 3) % 4, (y + 2) % 4
    zp, zm = (z + 1) % 16, (z + 15) % 16
    z4p, z4m = (z + 4) % 16, (z + 12) % 16
    Dxp, Dxm = dev(xp, y, z, c), dev(xm, y, z, c)
    Dyp, Dym = dev(x, yp, z, c), dev(x, ym, z, c)
    Dzp, Dzm = dev(x, y, zp, c), dev(x, y, zm, c)
    D4p, D4m = dev(x, y, z4p, c), dev(x, y, z4m, c)
    Dpart = dev(x, y, z, oc)
    ring = [(yt, cc) for yt in (yp, ym, yo) for cc in (c, oc)] + [(y, oc)]

    barrier = pltpu.get_barrier_semaphore()
    peers = [Dxp, Dxm, Dzp, Dzm, D4p, D4m] + [dev(x, yt, z, cc) for yt, cc in ring]
    for peer in peers:
        pl.semaphore_signal(barrier, inc=1, device_id=peer, device_id_type=MESH)

    for r in range(CHUNKS):
        fold = None
        for g in range(4):
            v = hid[pl.ds(ROWS * r, ROWS), pl.ds(128 * g, 128)].astype(F32)
            fold = v * v if fold is None else fold + v * v
        S1[2 * y + c, :, pl.ds(ROWS * r, ROWS)] = jnp.sum(fold.T, axis=0, keepdims=True)

    pl.semaphore_wait(barrier, len(peers))

    cs = (l // 2) % 2
    lcz = 2 * (l // 4) + l % 2
    row0 = pl.multiple_of(16 * c, 16)

    def pieces(yt):
        a0 = pl.multiple_of(1024 * yt, 512)
        b0 = pl.multiple_of(128 * yt, 128)
        rows = pl.ds(row0, 16)
        return (
            (qw.at[:, pl.ds(a0, 512)], Z.at[lcz, y, h, rows, pl.ds(0, 512)]),
            (kw.at[:, pl.ds(b0, 128)], Z.at[lcz, y, h, rows, pl.ds(512, 128)]),
            (vw.at[:, pl.ds(b0, 128)], Z.at[lcz, y, h, rows, pl.ds(640, 128)]),
            (qw.at[:, pl.ds(pl.multiple_of(a0 + 512, 512), 512)], Z.at[lcz, y, h, rows, pl.ds(768, 512)]),
        )

    for i, yt in enumerate((yp, ym, yo)):
        for src, dst in pieces(yt):
            remote(src, dst, w1s.at[i], zr.at[lcz, h, y], dev(x, yt, z, cs)).start()

    @pl.when(cs == c)
    def _():
        for src, dst in pieces(y):
            pltpu.make_async_copy(src, dst, zr.at[lcz, h, y]).start()

    @pl.when(cs != c)
    def _():
        for src, dst in pieces(y):
            remote(src, dst, w1s.at[3], zr.at[lcz, h, y], Dpart).start()

    for i, (yt, cc) in enumerate(ring):
        remote(S1.at[2 * y + c], S1.at[2 * y + c], s1s.at[i], s1r.at[2 * y + c], dev(x, yt, z, cc)).start()

    col0 = pl.multiple_of(512 * h, 512)

    def slot(s):
        ls, hs = s % 8, s // 8
        return (ls // 2) % 2 == c, 2 * (ls // 4) + ls % 2, hs

    def zcopy(lc, hs, sub, d):
        ref = Z.at[lc, sub, hs]
        return remote(ref, ref, zs.at[d, lc, hs, sub], zr.at[lc, hs, sub], Dzp if d == 0 else Dzm)

    def xcopy(lc, hs, sub, d):
        return remote(
            Z.at[lc, sub, hs, :, pl.ds(col0, 768)], W.at[x, lc, sub, hs], xs.at[d, lc, hs, sub], xr.at[d, lc, hs, sub],
            Dxp if d == 0 else Dxm,
        )

    def xfcopy(lc, hs, sub, d):
        ref = W.at[xm if d == 0 else xp, lc, sub, hs]
        return remote(ref, ref, xs.at[2, lc, hs, sub], xr.at[2, lc, hs, sub], Dxp if d == 0 else Dxm)

    def process(s, dirs):
        mine, lc, hs = slot(s)

        @pl.when(mine)
        def _():
            def body(sub, carry):
                zcopy(lc, hs, sub, 0).wait_recv()
                for d in dirs:
                    zcopy(lc, hs, sub, d).start()
                for d in (0, 1):
                    xcopy(lc, hs, sub, d).start()
                return carry

            lax.fori_loop(0, 4, body, 0)

    def xforward(s):
        mine, lc, hs = slot(s)

        @pl.when(mine)
        def _():
            def body(i, carry):
                xcopy(lc, hs, i, 0).wait_recv()
                xfcopy(lc, hs, i, 0).start()
                xcopy(lc, hs, i + 2, 1).wait_recv()
                xfcopy(lc, hs, i + 2, 1).start()
                return carry

            lax.fori_loop(0, 2, body, 0)

    def zround(k):
        process((z + 16 - k) % 16, (0,) if k < 8 else ())
        if k < 8:
            process((z + k) % 16, (1,) if k < 7 else ())

    def xround(k):
        xforward((z + 16 - k) % 16)
        if 0 < k < 8:
            xforward((z + k) % 16)

    def hcopy(cls, r, d):
        hh = h if cls == 0 else 1 - h
        ref = H.at[y, hh, r]
        return remote(ref, ref, hs_.at[cls, d, r], hr.at[cls, d, r], Dyp if d == 0 else Dym)

    def hfcopy(cls, r):
        hh = h if cls == 0 else 1 - h
        ref = H.at[ym if r % 2 == 0 else yp, hh, r]
        return remote(ref, ref, hfs.at[cls, r], hfr.at[cls, r], Dyp if r % 2 == 0 else Dym)

    def leg1(r):
        return remote(H.at[y, h, r], R.at[r], rs.at[r], rr.at[r], D4p if r % 2 == 0 else D4m)

    def leg2(r):
        origin = z4m if r % 2 == 0 else z4p
        return remote(R.at[r], H.at[y, origin // 8, r], ops.at[r], opr.at[r], D4p if r % 2 == 0 else D4m)

    def relay(r):
        leg1(r).wait_recv()
        leg2(r).start()

    def spread(cls, r):
        hcopy(cls, r, 0).start()
        hcopy(cls, r, 1).start()

    def opposite(r):
        leg2(r).wait_recv()
        spread(1, r)

    def yforward(cls, r):
        hcopy(cls, r, r % 2).wait_recv()
        hfcopy(cls, r).start()

    def yfinish(cls, r):
        hcopy(cls, r, 1 - r % 2).wait_recv()
        hfcopy(cls, r).wait_recv()

    def s2copy(i):
        return remote(S2.at[i], S2.at[i + 1], s2s.at[i], s2r.at[i], D4p)

    process(z, (0, 1))

    for yt, cc in ring:
        remote(S1.at[2 * yt + cc], S1.at[2 * yt + cc], s1s.at[0], s1r.at[2 * yt + cc], Dpart).wait_recv()
    part = S1[0]
    for i in range(1, 8):
        part = part + S1[i]
    S2[0] = part
    s2copy(0).start()

    zround(1)
    xround(0)
    s2copy(0).wait_recv()
    s2copy(1).start()
    zround(2)
    xround(1)
    s2copy(1).wait_recv()
    total = S2[0] + S2[2]
    for r in range(CHUNKS):
        wide = jnp.broadcast_to(total[:, ROWS * r : ROWS * (r + 1)], (ROWS, ROWS)).T
        inv = lax.rsqrt(wide / D + 1e-05)
        for g in range(4):
            v = hid[pl.ds(ROWS * r, ROWS), pl.ds(128 * g, 128)].astype(F32)
            H[y, h, r, :, pl.ds(128 * g, 128)] = (v * inv * gain[:, pl.ds(128 * g, 128)].astype(F32)).astype(BF16)
        leg1(r).start()
        spread(0, r)

    zround(3)
    xround(2)
    yforward(0, 0)
    yforward(0, 1)
    zround(4)
    xround(3)
    yforward(0, 2)
    yforward(0, 3)
    relay(0)
    relay(1)
    zround(5)
    xround(4)
    zround(6)
    xround(5)
    relay(2)
    relay(3)
    zround(7)
    xround(6)
    opposite(0)
    opposite(1)
    zround(8)
    xround(7)
    yforward(1, 0)
    yforward(1, 1)
    xround(8)

    def wfinish(i, carry):
        lc, hs = i // 2, i % 2
        for sub in range(4):
            if sub < 2:
                xcopy(lc, hs, sub, 1).wait_recv()
            else:
                xcopy(lc, hs, sub, 0).wait_recv()
            xfcopy(lc, hs, sub, 0).wait_recv()
        return carry

    lax.fori_loop(0, 8, wfinish, 0)

    off_own = 256 * h + 256 * c
    off_oth = 256 * h + 256 * oc
    off_kv = 512 * (1 - h)

    def group(r, off):
        acc = None
        for rel in range(4):
            yb = (x + rel) % 4
            lhs = jnp.concatenate([H[yb, 0, r], H[yb, 1, r]], axis=1)
            if rel == 0:
                rhs = Z[:, :, :, :, pl.ds(pl.multiple_of(512 * h + off, 256), 256)]
            else:
                rhs = W[yb, :, :, :, :, pl.ds(pl.multiple_of(off, 256), 256)]
            prod = jnp.dot(lhs, rhs.reshape(1024, 256), preferred_element_type=F32)
            acc = prod if acc is None else acc + prod
        return acc

    def ecopy(r):
        return remote(SB.at[r], RB.at[r], es.at[r], er.at[r], Dpart)

    def project(r):
        yfinish(0, r)
        yfinish(1, r)
        SB[r, :, pl.ds(0, 256)] = group(r, off_oth)
        kv = group(r, off_kv)
        SB[r, :, pl.ds(256, 256)] = kv
        ecopy(r).start()
        PO[r, :, pl.ds(256, 256)] = kv
        PO[r, :, pl.ds(0, 256)] = group(r, off_own)

    def rotated(v, r):
        co = cos[pl.ds(ROWS * r, ROWS), :]
        si = sin[pl.ds(ROWS * r, ROWS), :]
        return (v * co + pltpu.roll(v, 64, 1) * si).astype(BF16)

    def attend(r):
        ecopy(r).wait_recv()

        def summed(j):
            return PO[r, :, pl.ds(128 * j, 128)] + RB[r, :, pl.ds(128 * j, 128)]

        KB[pl.ds(ROWS * r, ROWS), :] = rotated(summed(2), r)
        VB[pl.ds(ROWS * r, ROWS), :] = summed(3).astype(BF16)
        n = ROWS * (r + 1)
        keys = KB[pl.ds(0, n), :]
        vals = VB[pl.ds(0, n), :]
        row = lax.broadcasted_iota(jnp.int32, (ROWS, n), 0) + ROWS * r
        col = lax.broadcasted_iota(jnp.int32, (ROWS, n), 1)
        for j in range(2):
            query = rotated(summed(j), r)
            sc = lax.dot_general(query, keys, (((1,), (1,)), ((), ())), preferred_element_type=F32) * SCALE
            sc = jnp.where(col <= row, sc, F32(-1e30))
            top = jnp.max(sc, axis=1, keepdims=True)
            ex = jnp.exp(sc - top)
            probs = (ex / jnp.sum(ex, axis=1, keepdims=True)).astype(BF16)
            out[pl.ds(ROWS * r, ROWS), pl.ds(HD * j, HD)] = jnp.dot(probs, vals, preferred_element_type=F32).astype(BF16)

    project(0)
    project(1)
    opposite(2)
    opposite(3)
    attend(0)
    yforward(1, 2)
    yforward(1, 3)
    attend(1)
    project(2)
    project(3)
    attend(2)
    attend(3)

    for i, yt in enumerate((yp, ym, yo)):
        ref = Z.at[0, 0, 0, pl.ds(0, 16)]
        remote(ref, ref, w1s.at[i], s1r.at[0], Dpart).wait_send()

    @pl.when(cs != c)
    def _():
        ref = Z.at[0, 0, 0, pl.ds(0, 16)]
        remote(ref, ref, w1s.at[3], s1r.at[0], Dpart).wait_send()

    for i in range(7):
        remote(S1.at[0], S1.at[0], s1s.at[i], s1r.at[0], Dpart).wait_send()
    for i in range(2):
        s2copy(i).wait_send()

    def zdone(k, carry):
        mine, lc, hs = slot((z + 16 - k) % 16)

        @pl.when(mine)
        def _():
            for sub in range(4):
                zcopy(lc, hs, sub, 0).wait_send()

        return carry

    lax.fori_loop(0, 8, zdone, 0)

    def zdone_down(k, carry):
        mine, lc, hs = slot((z + k) % 16)

        @pl.when(mine)
        def _():
            for sub in range(4):
                zcopy(lc, hs, sub, 1).wait_send()

        return carry

    lax.fori_loop(0, 7, zdone_down, 0)

    def xdone(i, carry):
        lc, hs = i // 2, i % 2
        for sub in range(4):
            xcopy(lc, hs, sub, 0).wait_send()
            xcopy(lc, hs, sub, 1).wait_send()
            xfcopy(lc, hs, sub, 0).wait_send()
        return carry

    lax.fori_loop(0, 8, xdone, 0)
    for r in range(CHUNKS):
        leg1(r).wait_send()
        leg2(r).wait_send()
        ecopy(r).wait_send()
        for cls in (0, 1):
            hcopy(cls, r, 0).wait_send()
            hcopy(cls, r, 1).wait_send()
            hfcopy(cls, r).wait_send()


def on_device(hidden_in, norm_gain, q_weight, k_weight, v_weight):
    cos, sin = tables()
    dma = pltpu.SemaphoreType.DMA
    vmem = pltpu.VMEM
    return pl.pallas_call(
        kernel,
        out_shape=jax.ShapeDtypeStruct((SEQ, 256), BF16),
        in_specs=[pl.BlockSpec(memory_space=pltpu.VMEM)] * 7,
        out_specs=pl.BlockSpec(memory_space=pltpu.VMEM),
        scratch_shapes=[
            vmem((4, 4, 2, 32, 1280), BF16),
            vmem((4, 4, 4, 2, 32, 768), BF16),
            vmem((4, 2, CHUNKS, ROWS, BLK), BF16),
            vmem((CHUNKS, ROWS, BLK), BF16),
            vmem((8, 1, SEQ), F32),
            vmem((3, 1, SEQ), F32),
            vmem((CHUNKS, ROWS, 512), F32),
            vmem((CHUNKS, ROWS, 512), F32),
            vmem((CHUNKS, ROWS, 512), F32),
            vmem((SEQ, HD), BF16),
            vmem((SEQ, HD), BF16),
            dma((4, 2, 4)),
            dma((2, 4, 2, 4)),
            dma((3, 4, 2, 4)),
            dma((3, 4, 2, 4)),
            dma((4,)),
            dma((8,)),
            dma((7,)),
            dma((2,)),
            dma((2,)),
            dma((CHUNKS,)),
            dma((CHUNKS,)),
            dma((CHUNKS,)),
            dma((CHUNKS,)),
            dma((2, 2, CHUNKS)),
            dma((2, 2, CHUNKS)),
            dma((2, CHUNKS)),
            dma((2, CHUNKS)),
            dma((CHUNKS,)),
            dma((CHUNKS,)),
        ],
        compiler_params=pltpu.CompilerParams(
            collective_id=0, has_side_effects=True, vmem_limit_bytes=48 * 1024 * 1024
        ),
    )(hidden_in, norm_gain.reshape(1, -1), q_weight, k_weight, v_weight, jnp.asarray(cos), jnp.asarray(sin))


def solution(mesh):
    placed = (
        P("batch", "tensor"),
        P("tensor"),
        P(("batch", "tensor"), None),
        P(("batch", "tensor"), None),
        P(("batch", "tensor"), None),
    )
    return jax.shard_map(
        on_device, mesh=mesh, in_specs=placed, out_specs=P("batch", "tensor"), check_vma=False
    )
```

time: 905 us -> 135 us (0.15)
  the two profiles are of different devices: /device:TPU:24 before, /device:TPU:41 now
where the time goes in v1:
time: 135 us
  Pallas kernels  128 us (95%)
  local copies, waits for them, and re-layouts  6.66 us (5%)
    pallas_call x1, Pallas kernels, on_device(): pl.pallas_call(kernel, out_shape=jax.ShapeDtypeStruct((SEQ, 256), BF16),...  128 us
    unnamed x13, local copies, waits for them, and re-layouts  5.98 us

profile of v1, /device:TPU:41, one launch (start us, length us, event | category | flops | bytes accessed | tf_op | source)
XLA Modules:
  0.0 134.7 jit_solution(16493512807953815603)
XLA Ops:
  0.0 0.7 reshape.3.gain
  0.7 0.0 copy-start
  0.7 1.0 copy-done
  1.7 0.0 copy-start.1
  1.7 0.9 copy-done.1
  2.7 0.0 copy-start.2
  2.7 0.9 copy-done.2
  3.6 0.0 copy-start.3
  3.6 0.9 copy-done.3
  4.5 0.0 copy-start.4
  4.5 0.7 copy-done.4
  5.2 0.0 copy-start.5
  5.3 0.7 copy-done.5
  6.0 128.1 %shard_map.73 = bf16[512,256]{1,0:T(8,128)(2,1)S(1)} custom-call(bf16[512,512]{1,0:T(8,128)(2,1)S(1)} %copy-done, bf16[1,512]{1,0:T(2,128)(2,1)S(1)} %reshape.3.gain, bf16[16,4096]{1,0:T(8,128)(2,1)S(1)} %copy-done.3, bf16[16,512]{1,0:T(8,128)(2,1)S(1)} %copy-done.4, bf16[16,512]{1,0:T(8,128)(2,1)S(1)} %copy-done.5, f32[512,128]{1,0:T(8,128)S(1)} %copy-done.2, ...), custom_call_target="tpu_custom_call" | custom-call | tf_op jit(solution)/shard_map/pallas_call | solution.py:406
  134.0 0.7 copy.9
Async XLA Ops:
  0.7 1.0 copy-start
  1.7 0.9 copy-start.1
  2.7 0.9 copy-start.2
  3.6 0.9 copy-start.3
  4.5 0.7 copy-start.4
  5.2 0.7 copy-start.5

commit v2 on v0

v2 whole, which is shorter than its diff:
```python
import functools

import jax
import jax.numpy as jnp
import numpy as np
from jax import lax
from jax.experimental import pallas as pl
from jax.experimental.pallas import tpu as pltpu
from jax.sharding import PartitionSpec as P

MESH = pl.DeviceIdType.MESH
BF16 = jnp.bfloat16
F32 = jnp.float32
HD = 128
SEQ = 512
ROWS = 128
CHUNKS = SEQ // ROWS
BLK = 512
D = 8192
PIECE = 32
PER = ROWS // PIECE
SCHEDULE = (
    ('y',),
    ('z', 0),
    ('t',),
    ('h',),
    ('z', 1),
    ('z', 2),
    ('x', 0),
    ('z', 3),
    ('z', 4),
    ('x', 1),
    ('z', 5),
    ('x', 2),
    ('z', 6),
    ('x', 3),
    ('z', 7),
    ('z', 8),
    ('x', 4),
    ('s', 0, 16),
    ('x', 5),
    ('x', 6),
    ('o', 0, 1),
    ('x', 7),
    ('o', 1, 3),
    ('x', 8),
    ('o', 3, 6),
    ('f',),
    ('n',),
    ('o', 6, 9),
    ('p', 0),
    ('o', 9, 10),
    ('a', 0),
    ('o', 10, 11),
    ('p', 1),
    ('o', 11, 12),
    ('a', 1),
    ('o', 12, 13),
    ('p', 2),
    ('o', 13, 14),
    ('a', 2),
    ('o', 14, 16),
    ('p', 3),
    ('a', 3),
)
SCALE = 1.0 / float(np.sqrt(np.float32(HD)))


def tables():
    position = np.arange(SEQ, dtype=np.float32)
    half = HD // 2
    freqs = np.power(np.float32(500000.0), -(np.arange(half, dtype=np.float32) * np.float32(2.0)) / np.float32(HD))
    angles = (position[:, None] * freqs[None, :].astype(np.float32)).astype(np.float32).astype(np.float64)
    cosine = np.cos(angles).astype(np.float32)
    sine = np.sin(angles).astype(np.float32)
    return np.concatenate([cosine, cosine], axis=1), np.concatenate([-sine, sine], axis=1)


def remote(src, dst, send, recv, device):
    return pltpu.make_async_remote_copy(
        src_ref=src, dst_ref=dst, send_sem=send, recv_sem=recv, device_id=device, device_id_type=MESH
    )


def kernel(
    hid_in, gain, qw, kw, vw, cos_in, sin_in, out,
    cos, sin, Z, W, H, HX, S1, ST, IV, NB, PO, SB, RB, KB, VB,
    ld, zr, zs, xr, xs, xfs, hx, w1s, s1r, s1s, s2r, s2s, opr, ops, hr, hs_, gr, gs, er, es, far,
):
    b = lax.axis_index("batch")
    t = lax.axis_index("tensor")
    x, l = b // 8, b % 8
    y, h, c = t // 4, (t // 2) % 2, t % 2
    z = 8 * h + l
    oc = 1 - c

    def dev(xx, yy, zz, cc):
        return (8 * xx + zz % 8, 4 * yy + 2 * (zz // 8) + cc)

    xp, xm = (x + 1) % 4, (x + 3) % 4
    yp, ym, yo = (y + 1) % 4, (y + 3) % 4, (y + 2) % 4
    zp, zm, zo = (z + 1) % 16, (z + 15) % 16, (z + 8) % 16
    z4p, z4m = (z + 4) % 16, (z + 12) % 16
    Dxp, Dxm = dev(xp, y, z, c), dev(xm, y, z, c)
    Dy = (dev(x, yp, z, c), dev(x, ym, z, c), dev(x, yo, z, c))
    Dzp, Dzm, Dzo = dev(x, y, zp, c), dev(x, y, zm, c), dev(x, y, zo, c)
    D4p, D4m = dev(x, y, z4p, c), dev(x, y, z4m, c)
    Dpart = dev(x, y, z, oc)
    ring = [(yt, cc) for yt in (yp, ym, yo) for cc in (c, oc)] + [(y, oc)]

    loads = [
        pltpu.make_async_copy(src, dst, ld.at[i])
        for i, (src, dst) in enumerate(
            [(hid_in.at[pl.ds(ROWS * r, ROWS)], H.at[y, h, r]) for r in range(CHUNKS)] + [(cos_in, cos), (sin_in, sin)]
        )
    ]
    for load in loads:
        load.start()

    barrier = pltpu.get_barrier_semaphore()
    peers = [Dzp, Dzm] + [dev(x, yt, z, cc) for yt, cc in ring]
    for cc in (c, oc):
        peers += [dev(xp, y, z, cc), dev(xm, y, z, cc), dev(x, y, z4p, cc), dev(x, y, z4m, cc)]
    for peer in peers:
        pl.semaphore_signal(barrier, inc=1, device_id=peer, device_id_type=MESH)

    S1[2 * y + c, 1] = gain[...].astype(F32)
    for r in range(CHUNKS):
        loads[r].wait()
        fold = None
        for g in range(4):
            v = H[y, h, r, :, pl.ds(128 * g, 128)].astype(F32)
            fold = v * v if fold is None else fold + v * v
        S1[2 * y + c, 0, :, pl.ds(ROWS * r, ROWS)] = jnp.sum(fold.T, axis=0, keepdims=True)

    pl.semaphore_wait(barrier, len(peers))
    pl.semaphore_signal(far, inc=1, device_id=D4m, device_id_type=MESH)

    row0 = pl.multiple_of(16 * c, 16)

    def pieces(yt):
        a0 = pl.multiple_of(1024 * yt, 512)
        b0 = pl.multiple_of(128 * yt, 128)
        rows = pl.ds(row0, 16)
        return (
            (qw.at[:, pl.ds(a0, 512)], Z.at[l, y, h, rows, pl.ds(0, 512)]),
            (kw.at[:, pl.ds(b0, 128)], Z.at[l, y, h, rows, pl.ds(512, 128)]),
            (vw.at[:, pl.ds(b0, 128)], Z.at[l, y, h, rows, pl.ds(640, 128)]),
            (qw.at[:, pl.ds(pl.multiple_of(a0 + 512, 512), 512)], Z.at[l, y, h, rows, pl.ds(768, 512)]),
        )

    for i, yt in enumerate((yp, ym, yo)):
        for src, dst in pieces(yt):
            remote(src, dst, w1s.at[i], zr.at[l, h, y], dev(x, yt, z, 0)).start()

    @pl.when(c == 0)
    def _():
        for src, dst in pieces(y):
            pltpu.make_async_copy(src, dst, zr.at[l, h, y]).start()

    @pl.when(c == 1)
    def _():
        for src, dst in pieces(y):
            remote(src, dst, w1s.at[3], zr.at[l, h, y], Dpart).start()

    for i, (yt, cc) in enumerate(ring):
        remote(S1.at[2 * y + c], S1.at[2 * y + c], s1s.at[i], s1r.at[2 * y + c], dev(x, yt, z, cc)).start()

    col0 = pl.multiple_of(512 * h, 512)

    def slot(s):
        ls, hs = s % 8, s // 8
        return (ls // 2) % 2, 2 * (ls // 4) + ls % 2, hs

    def need(s, k, d):
        sl, hs = s % 8, s // 8
        if d == 0:
            return sl + k < 8, 1 - hs
        return jnp.logical_and(k <= sl, sl != 7), jnp.where(sl == 7, hs, 1 - hs)

    def zeach(s, k, d, sub, act):
        ls, hs = s % 8, s // 8
        both, half = need(s, k, d)
        sems = (zs.at[d, ls, hs, sub], zr.at[ls, hs, sub], Dzp if d == 0 else Dzm)

        @pl.when(both)
        def _():
            ref = Z.at[ls, sub, hs]
            act(remote(ref, ref, *sems))

        @pl.when(jnp.logical_not(both))
        def _():
            ref = Z.at[ls, sub, hs, :, pl.ds(pl.multiple_of(512 * half, 512), 768)]
            act(remote(ref, ref, *sems))

    def start(copy):
        copy.start()

    def wait_recv(copy):
        copy.wait_recv()

    def wait_send(copy):
        copy.wait_send()

    def xcopy(s, sub, d):
        cc, lc, hs = slot(s)
        ls = s % 8
        return remote(
            Z.at[ls, sub, hs, :, pl.ds(col0, 768)], W.at[x, lc, sub, hs], xs.at[d, ls, hs, sub], xr.at[d, lc, hs, sub],
            dev((xp, xm, x)[d], y, z, cc),
        )

    def xfcopy(lc, hs, sub, d):
        ref = W.at[xm if d == 0 else xp, lc, sub, hs]
        return remote(ref, ref, xfs.at[lc, hs, sub], xr.at[3, lc, hs, sub], Dxp if d == 0 else Dxm)

    def zstep(k, d, sub):
        s = (z + 16 - k) % 16 if d == 0 else (z + k) % 16
        cc, lc, hs = slot(s)
        if k == 0:
            ref = Z.at[s % 8, sub, hs]
            remote(ref, ref, zs.at[0, s % 8, hs, sub], zr.at[s % 8, hs, sub], Dzp).wait_recv()
            zeach(s, 1, 0, sub, start)
            zeach(s, 1, 1, sub, start)
        else:
            zeach(s, k, d, sub, wait_recv)
            if k < 8 - d:
                zeach(s, k + 1, d, sub, start)
        xcopy(s, sub, 0).start()
        xcopy(s, sub, 1).start()

        @pl.when(cc == 1)
        def _():
            xcopy(s, sub, 2).start()

        @pl.when(cc == 0)
        def _():
            pltpu.make_async_copy(
                Z.at[s % 8, sub, hs, :, pl.ds(col0, 768)], W.at[x, lc, sub, hs], xr.at[2, lc, hs, sub]
            ).start()

    def xstep(k, d, sub, way):
        s = (z + 16 - k) % 16 if d == 0 else (z + k) % 16
        cc, lc, hs = slot(s)

        @pl.when(cc == c)
        def _():
            xcopy(s, sub, way).wait_recv()
            xfcopy(lc, hs, sub, way).start()

    def zround(k):
        @pl.when(c == 0)
        def _():
            def body(sub, carry):
                zstep(k, 0, sub)
                if 0 < k < 8:
                    zstep(k, 1, sub)
                return carry

            lax.fori_loop(0, 4, body, 0)

    def xround(k):
        def body(i, carry):
            for j in range(2):
                xstep(k, 0, 2 * i + j, j)
                if 0 < k < 8:
                    xstep(k, 1, 2 * i + j, j)
            return carry

        lax.fori_loop(0, 2, body, 0)

    def hcopy(r, d):
        ref = H.at[y, h, r]
        return remote(ref, ref, hs_.at[d, r], hr.at[d, r], Dy[d])

    def hwait(r, d):
        hcopy(r, d).wait_recv()

    def ocopy(p, cc):
        part = (p // PER, pl.ds(PIECE * (p % PER), PIECE))
        src = H.at[y, h, part[0], part[1]] if cc == 1 else HX.at[part[0], part[1]]
        return remote(src, H.at[y, h, part[0], part[1]], ops.at[cc, p], opr.at[p], dev(x, y, zo, cc))

    pushed = remote(H.at[y, h], HX, hx.at[0], hx.at[1], Dpart)

    def push():
        @pl.when(c == 0)
        def _():
            pushed.start()

        @pl.when(c == 1)
        def _():
            pushed.wait_recv()

    def across(first, last):
        @pl.when(c == 1)
        def _():
            def body(p, carry):
                ocopy(p, 1).start()
                ocopy(p, 0).start()
                return carry

            lax.fori_loop(first, last, body, 0)

    def gcopy(p, d):
        ref = H.at[y, 1 - h, p // PER, pl.ds(PIECE * (p % PER), PIECE)]
        return remote(ref, ref, gs.at[d, p], gr.at[d, p], Dy[d])

    def opposite(p):
        ocopy(p, 1).wait_recv()
        for d in range(3):
            gcopy(p, d).start()

    s2copy = remote(ST.at[0], ST.at[1], s2s.at[0], s2r.at[0], Dzo)

    def stats():
        for yt, cc in ring:
            remote(S1.at[2 * yt + cc], S1.at[2 * yt + cc], s1s.at[0], s1r.at[2 * yt + cc], Dpart).wait_recv()
        part = S1[0, 0]
        for i in range(1, 8):
            part = part + S1[i, 0]
        ST[0, 0] = part
        for i in range(4):
            ST[0, 1 + i] = S1[2 * i + c, 1]
        pl.semaphore_wait(far, 1)
        s2copy.start()

    def scales():
        s2copy.wait_recv()
        total = ST[0, 0] + ST[1, 0]
        for r in range(CHUNKS):
            wide = jnp.broadcast_to(total[:, ROWS * r : ROWS * (r + 1)], (ROWS, ROWS)).T
            IV[r] = lax.rsqrt(wide / D + 1e-05)

    def normalize(r):
        for rel in range(4):
            yb = (x + rel) % 4
            for hb in range(2):
                own = jnp.where(h == hb, 0, 1)
                for g in range(4):
                    v = H[yb, hb, r, :, pl.ds(128 * g, 128)].astype(F32)
                    scale = ST[own, 1 + yb, :, pl.ds(128 * g, 128)]
                    NB[:, pl.ds(1024 * rel + 512 * hb + 128 * g, 128)] = (v * IV[r] * scale).astype(BF16)

    off_own = 256 * h + 256 * c
    off_oth = 256 * h + 256 * oc
    off_kv = 512 * (1 - h)

    def group(r, off):
        acc = None
        for rel in range(4):
            yb = (x + rel) % 4
            lhs = NB[:, pl.ds(1024 * rel, 1024)]
            rhs = W[yb, :, :, :, :, pl.ds(pl.multiple_of(off, 256), 256)]
            prod = jnp.dot(lhs, rhs.reshape(1024, 256), preferred_element_type=F32)
            acc = prod if acc is None else acc + prod
        return acc

    def ecopy(r):
        return remote(SB.at[r], RB.at[r], es.at[r], er.at[r], Dpart)

    def project(r):
        for d in range(3):
            hwait(r, d)
            for p in range(PER * r, PER * (r + 1)):
                gcopy(p, d).wait_recv()
        normalize(r)
        SB[r, :, pl.ds(0, 256)] = group(r, off_oth)
        kv = group(r, off_kv)
        SB[r, :, pl.ds(256, 256)] = kv
        ecopy(r).start()
        PO[r, :, pl.ds(256, 256)] = kv
        PO[r, :, pl.ds(0, 256)] = group(r, off_own)

    def rotated(v, r):
        co = cos[pl.ds(ROWS * r, ROWS), :]
        si = sin[pl.ds(ROWS * r, ROWS), :]
        return (v * co + pltpu.roll(v, 64, 1) * si).astype(BF16)

    def attend(r):
        ecopy(r).wait_recv()

        def summed(j):
            return PO[r, :, pl.ds(128 * j, 128)] + RB[r, :, pl.ds(128 * j, 128)]

        KB[pl.ds(ROWS * r, ROWS), :] = rotated(summed(2), r)
        VB[pl.ds(ROWS * r, ROWS), :] = summed(3).astype(BF16)
        n = ROWS * (r + 1)
        keys = KB[pl.ds(0, n), :]
        vals = VB[pl.ds(0, n), :]
        row = lax.broadcasted_iota(jnp.int32, (ROWS, n), 0) + ROWS * r
        col = lax.broadcasted_iota(jnp.int32, (ROWS, n), 1)
        for j in range(2):
            query = rotated(summed(j), r)
            sc = lax.dot_general(query, keys, (((1,), (1,)), ((), ())), preferred_element_type=F32) * SCALE
            sc = jnp.where(col <= row, sc, F32(-1e30))
            top = jnp.max(sc, axis=1, keepdims=True)
            ex = jnp.exp(sc - top)
            probs = (ex / jnp.sum(ex, axis=1, keepdims=True)).astype(BF16)
            out[pl.ds(ROWS * r, ROWS), pl.ds(HD * j, HD)] = jnp.dot(probs, vals, preferred_element_type=F32).astype(BF16)

    def wfinish():
        def body(i, carry):
            lc, hs = i // 2, i % 2
            for sub in range(4):
                source = 8 * hs + 4 * (lc // 2) + 2 * c + lc % 2
                xcopy(source, sub, 1 - sub % 2).wait_recv()
                xcopy(source, sub, 2).wait_recv()
                xfcopy(lc, hs, sub, 0).wait_recv()
            return carry

        lax.fori_loop(0, 8, body, 0)

    def rope_tables():
        loads[CHUNKS].wait()
        loads[CHUNKS + 1].wait()

    for step in SCHEDULE:
        name, args = step[0], step[1:]
        if name == "z":
            zround(*args)
        elif name == "x":
            xround(*args)
        elif name == "t":
            stats()
        elif name == "n":
            scales()
        elif name == "y":
            for r in range(CHUNKS):
                for d in range(3):
                    hcopy(r, d).start()
        elif name == "h":
            push()
        elif name == "s":
            across(*args)
        elif name == "o":
            for p in range(*args):
                opposite(p)
        elif name == "f":
            wfinish()
            rope_tables()
        elif name == "p":
            project(*args)
        else:
            attend(*args)

    piece16 = Z.at[0, 0, 0, pl.ds(0, 16)]
    for i in range(3):
        remote(piece16, piece16, w1s.at[i], s1r.at[0], Dpart).wait_send()

    @pl.when(c == 1)
    def _():
        remote(piece16, piece16, w1s.at[3], s1r.at[0], Dpart).wait_send()

    for i in range(7):
        remote(S1.at[0], S1.at[0], s1s.at[i], s1r.at[0], Dpart).wait_send()
    s2copy.wait_send()

    def zdone(d):
        def body(k, carry):
            s = (z + 16 - k) % 16 if d == 0 else (z + k) % 16
            for sub in range(4):
                zeach(s, k + 1, d, sub, wait_send)
            return carry

        lax.fori_loop(0, 8 - d, body, 0)

    @pl.when(c == 0)
    def _():
        pushed.wait_send()
        zdone(0)
        zdone(1)

        def xdone(s, carry):
            for sub in range(4):
                xcopy(s, sub, 0).wait_send()
                xcopy(s, sub, 1).wait_send()

                @pl.when(slot(s)[0] == 1)
                def _():
                    xcopy(s, sub, 2).wait_send()

            return carry

        lax.fori_loop(0, 16, xdone, 0)

    def xfdone(i, carry):
        for sub in range(4):
            xfcopy(i // 2, i % 2, sub, 0).wait_send()
        return carry

    lax.fori_loop(0, 8, xfdone, 0)
    for r in range(CHUNKS):
        ecopy(r).wait_send()
        for d in range(3):
            hcopy(r, d).wait_send()

    def pdone(p, carry):
        @pl.when(c == 1)
        def _():
            ocopy(p, 0).wait_send()
            ocopy(p, 1).wait_send()

        for d in range(3):
            gcopy(p, d).wait_send()
        return carry

    lax.fori_loop(0, PER * CHUNKS, pdone, 0)


def on_device(hidden_in, norm_gain, q_weight, k_weight, v_weight):
    cos, sin = tables()
    dma = pltpu.SemaphoreType.DMA
    vmem = pltpu.VMEM
    hbm = pl.BlockSpec(memory_space=pltpu.HBM)
    return pl.pallas_call(
        kernel,
        out_shape=jax.ShapeDtypeStruct((SEQ, 256), BF16),
        in_specs=[hbm, pl.BlockSpec(memory_space=vmem), hbm, hbm, hbm, hbm, hbm],
        out_specs=pl.BlockSpec(memory_space=vmem),
        scratch_shapes=[
            vmem((SEQ, HD), F32),
            vmem((SEQ, HD), F32),
            vmem((8, 4, 2, 32, 1280), BF16),
            vmem((4, 4, 4, 2, 32, 768), BF16),
            vmem((4, 2, CHUNKS, ROWS, BLK), BF16),
            vmem((CHUNKS, ROWS, BLK), BF16),
            vmem((8, 2, 1, SEQ), F32),
            vmem((2, 5, 1, SEQ), F32),
            vmem((CHUNKS, ROWS, ROWS), F32),
            vmem((ROWS, 8 * BLK), BF16),
            vmem((CHUNKS, ROWS, 512), F32),
            vmem((CHUNKS, ROWS, 512), F32),
            vmem((CHUNKS, ROWS, 512), F32),
            vmem((SEQ, HD), BF16),
            vmem((SEQ, HD), BF16),
            dma((CHUNKS + 2,)),
            dma((8, 2, 4)),
            dma((2, 8, 2, 4)),
            dma((4, 4, 2, 4)),
            dma((3, 8, 2, 4)),
            dma((4, 2, 4)),
            dma((2,)),
            dma((4,)),
            dma((8,)),
            dma((7,)),
            dma((1,)),
            dma((1,)),
            dma((PER * CHUNKS,)),
            dma((2, PER * CHUNKS)),
            dma((3, CHUNKS)),
            dma((3, CHUNKS)),
            dma((3, PER * CHUNKS)),
            dma((3, PER * CHUNKS)),
            dma((CHUNKS,)),
            dma((CHUNKS,)),
            pltpu.SemaphoreType.REGULAR,
        ],
        compiler_params=pltpu.CompilerParams(
            collective_id=0, has_side_effects=True, vmem_limit_bytes=67043328
        ),
    )(hidden_in, norm_gain.reshape(1, -1), q_weight, k_weight, v_weight, jnp.asarray(cos), jnp.asarray(sin))


def solution(mesh):
    placed = (
        P("batch", "tensor"),
        P("tensor"),
        P(("batch", "tensor"), None),
        P(("batch", "tensor"), None),
        P(("batch", "tensor"), None),
    )
    return jax.shard_map(
        on_device, mesh=mesh, in_specs=placed, out_specs=P("batch", "tensor"), check_vma=False
    )
```

time: 905 us -> 123 us (0.14)
  the two profiles are of different devices: /device:TPU:24 before, /device:TPU:192 now
where the time goes in v2:
time: 123 us
  Pallas kernels  120 us (98%)
  local copies, waits for them, and re-layouts  2.93 us (2%)
    pallas_call x1, Pallas kernels, on_device(): pl.pallas_call(kernel, out_shape=jax.ShapeDtypeStruct((SEQ, 256), BF16),...  120 us

profile of v2, /device:TPU:192, one launch (start us, length us, event | category | flops | bytes accessed | tf_op | source)
XLA Modules:
  0.0 122.6 jit_solution(13115250958104950603)
XLA Ops:
  0.0 1.3 %reshape.3.gain = bf16[1,512]{1,0:T(2,128)(2,1)} reshape(bf16[512]{0:T(512)(128)(2,1)} %param.8) | data formatting | bytes 2048 | tf_op jit(solution)/shard_map/reshape | solution.py:562
  1.3 119.6 %shard_map.73 = bf16[512,256]{1,0:T(8,128)(2,1)} custom-call(bf16[512,512]{1,0:T(8,128)(2,1)} %hid_in.1, bf16[1,512]{1,0:T(2,128)(2,1)} %reshape.3.gain, bf16[16,4096]{1,0:T(8,128)(2,1)} %qw.1, bf16[16,512]{1,0:T(8,128)(2,1)} %kw.1, bf16[16,512]{1,0:T(8,128)(2,1)} %vw.1, f32[512,128]{1,0:T(8,128)} %constant.4.clone.cos_in, f32[512,128]{1,0:T(8,128)} %constant.5.clone.sin_in), custom_call_target="tpu_custom_call" | custom-call | tf_op jit(solution)/shard_map/pallas_call | solution.py:516
  120.9 1.7 %copy.9 = bf16[512,256]{1,0:T(8,128)(2,1)} copy(bf16[512,256]{1,0:T(8,128)(2,1)} %shard_map.73) | data formatting | bytes 524288

commit v3 on v2

--- a/solution.py
+++ b/solution.py
@@ -31,11 +31,11 @@
     ('z', 4),
     ('x', 1),
     ('z', 5),
+    ('z', 6),
     ('x', 2),
-    ('z', 6),
-    ('x', 3),
     ('z', 7),
     ('z', 8),
+    ('x', 3),
     ('x', 4),
     ('s', 0, 16),
     ('x', 5),
@@ -47,19 +47,25 @@
     ('o', 3, 6),
     ('f',),
     ('n',),
-    ('o', 6, 9),
+    ('o', 6, 8),
+    ('b', 0),
+    ('o', 8, 9),
+    ('b', 1),
+    ('o', 9, 10),
     ('p', 0),
-    ('o', 9, 10),
     ('a', 0),
     ('o', 10, 11),
+    ('b', 2),
+    ('o', 11, 12),
     ('p', 1),
-    ('o', 11, 12),
+    ('b', 3),
+    ('o', 12, 13),
     ('a', 1),
-    ('o', 12, 13),
+    ('o', 13, 14),
     ('p', 2),
-    ('o', 13, 14),
+    ('o', 14, 15),
     ('a', 2),
-    ('o', 14, 16),
+    ('o', 15, 16),
     ('p', 3),
     ('a', 3),
 )
@@ -124,7 +130,7 @@
     for peer in peers:
         pl.semaphore_signal(barrier, inc=1, device_id=peer, device_id_type=MESH)
 
-    S1[2 * y + c, 1] = gain[...].astype(F32)
+    S1[2 * y + c, 1] = gain[...].astype(F32).reshape(1, BLK)
     for r in range(CHUNKS):
         loads[r].wait()
         fold = None
@@ -259,7 +265,7 @@
 
             lax.fori_loop(0, 4, body, 0)
 
-    def xround(k):
+    def xround(k, first=0, last=2):
         def body(i, carry):
             for j in range(2):
                 xstep(k, 0, 2 * i + j, j)
@@ -267,7 +273,7 @@
                     xstep(k, 1, 2 * i + j, j)
             return carry
 
-        lax.fori_loop(0, 2, body, 0)
+        lax.fori_loop(first, last, body, 0)
 
     def hcopy(r, d):
         ref = H.at[y, h, r]
@@ -332,45 +338,50 @@
             wide = jnp.broadcast_to(total[:, ROWS * r : ROWS * (r + 1)], (ROWS, ROWS)).T
             IV[r] = lax.rsqrt(wide / D + 1e-05)
 
-    def normalize(r):
+    def normalize(r, hb, side):
         for rel in range(4):
             yb = (x + rel) % 4
-            for hb in range(2):
-                own = jnp.where(h == hb, 0, 1)
-                for g in range(4):
-                    v = H[yb, hb, r, :, pl.ds(128 * g, 128)].astype(F32)
-                    scale = ST[own, 1 + yb, :, pl.ds(128 * g, 128)]
-                    NB[:, pl.ds(1024 * rel + 512 * hb + 128 * g, 128)] = (v * IV[r] * scale).astype(BF16)
+            for g in range(4):
+                v = H[yb, hb, r, :, pl.ds(128 * g, 128)].astype(F32)
+                scale = ST[side, 1 + yb, :, pl.ds(128 * g, 128)]
+                NB[:, pl.ds(512 * rel + 128 * g, 128)] = (v * IV[r] * scale).astype(BF16)
 
     off_own = 256 * h + 256 * c
     off_oth = 256 * h + 256 * oc
     off_kv = 512 * (1 - h)
 
-    def group(r, off):
+    def group(hb, off):
         acc = None
         for rel in range(4):
             yb = (x + rel) % 4
-            lhs = NB[:, pl.ds(1024 * rel, 1024)]
-            rhs = W[yb, :, :, :, :, pl.ds(pl.multiple_of(off, 256), 256)]
-            prod = jnp.dot(lhs, rhs.reshape(1024, 256), preferred_element_type=F32)
+            lhs = NB[:, pl.ds(512 * rel, 512)]
+            rhs = W[yb, pl.ds(2 * hb, 2), :, :, :, pl.ds(pl.multiple_of(off, 256), 256)]
+            prod = jnp.dot(lhs, rhs.reshape(512, 256), preferred_element_type=F32)
             acc = prod if acc is None else acc + prod
         return acc
 
     def ecopy(r):
         return remote(SB.at[r], RB.at[r], es.at[r], er.at[r], Dpart)
 
+    def begin(r):
+        for d in range(3):
+            hwait(r, d)
+        normalize(r, h, 0)
+        SB[r, :, pl.ds(0, 256)] = group(h, off_oth)
+        SB[r, :, pl.ds(256, 256)] = group(h, off_kv)
+        PO[r, :, pl.ds(0, 256)] = group(h, off_own)
+
     def project(r):
         for d in range(3):
-            hwait(r, d)
             for p in range(PER * r, PER * (r + 1)):
                 gcopy(p, d).wait_recv()
-        normalize(r)
-        SB[r, :, pl.ds(0, 256)] = group(r, off_oth)
-        kv = group(r, off_kv)
+        normalize(r, 1 - h, 1)
+        SB[r, :, pl.ds(0, 256)] += group(1 - h, off_oth)
+        kv = SB[r, :, pl.ds(256, 256)] + group(1 - h, off_kv)
         SB[r, :, pl.ds(256, 256)] = kv
         ecopy(r).start()
         PO[r, :, pl.ds(256, 256)] = kv
-        PO[r, :, pl.ds(0, 256)] = group(r, off_own)
+        PO[r, :, pl.ds(0, 256)] += group(1 - h, off_own)
 
     def rotated(v, r):
         co = cos[pl.ds(ROWS * r, ROWS), :]
@@ -439,6 +450,8 @@
         elif name == "f":
             wfinish()
             rope_tables()
+        elif name == "b":
+            begin(*args)
         elif name == "p":
             project(*args)
         else:
@@ -528,7 +541,7 @@
             vmem((8, 2, 1, SEQ), F32),
             vmem((2, 5, 1, SEQ), F32),
             vmem((CHUNKS, ROWS, ROWS), F32),
-            vmem((ROWS, 8 * BLK), BF16),
+            vmem((ROWS, 4 * BLK), BF16),
             vmem((CHUNKS, ROWS, 512), F32),
             vmem((CHUNKS, ROWS, 512), F32),
             vmem((CHUNKS, ROWS, 512), F32),
@@ -559,7 +572,7 @@
         compiler_params=pltpu.CompilerParams(
             collective_id=0, has_side_effects=True, vmem_limit_bytes=67043328
         ),
-    )(hidden_in, norm_gain.reshape(1, -1), q_weight, k_weight, v_weight, jnp.asarray(cos), jnp.asarray(sin))
+    )(hidden_in, norm_gain, q_weight, k_weight, v_weight, jnp.asarray(cos), jnp.asarray(sin))
 
 
 def solution(mesh):

time: 123 us -> 118 us (0.959)
  the two profiles are of different devices: /device:TPU:192 before, /device:TPU:225 now
where the time goes in v3:
time: 118 us
  Pallas kernels  116 us (98%)
  local copies, waits for them, and re-layouts  1.67 us (1%)
    pallas_call x1, Pallas kernels, on_device(): pl.pallas_call(kernel, out_shape=jax.ShapeDtypeStruct((SEQ, 256), BF16),...  116 us

profile of v3, /device:TPU:225, one launch (start us, length us, event | category | flops | bytes accessed | tf_op | source)
XLA Modules:
  0.0 117.8 jit_solution(11034849072417349652)
XLA Ops:
  0.0 116.1 %shard_map.73 = bf16[512,256]{1,0:T(8,128)(2,1)} custom-call(bf16[512,512]{1,0:T(8,128)(2,1)} %hid_in.1, bf16[512]{0:T(512)(128)(2,1)} %gain.1, bf16[16,4096]{1,0:T(8,128)(2,1)} %qw.1, bf16[16,512]{1,0:T(8,128)(2,1)} %kw.1, bf16[16,512]{1,0:T(8,128)(2,1)} %vw.1, f32[512,128]{1,0:T(8,128)} %constant.4.clone.cos_in, f32[512,128]{1,0:T(8,128)} %constant.5.clone.sin_in), custom_call_target="tpu_custom_call" | custom-call | tf_op jit(solution)/shard_map/pallas_call | solution.py:529
  116.2 1.7 %copy.9 = bf16[512,256]{1,0:T(8,128)(2,1)} copy(bf16[512,256]{1,0:T(8,128)(2,1)} %shard_map.73) | data formatting | bytes 524288

commit v4 on v3

--- a/solution.py
+++ b/solution.py
@@ -63,9 +63,8 @@
     ('a', 1),
     ('o', 13, 14),
     ('p', 2),
-    ('o', 14, 15),
+    ('o', 14, 16),
     ('a', 2),
-    ('o', 15, 16),
     ('p', 3),
     ('a', 3),
 )
@@ -314,7 +313,7 @@
 
     def opposite(p):
         ocopy(p, 1).wait_recv()
-        for d in range(3):
+        for d in (2, 0, 1):
             gcopy(p, d).start()
 
     s2copy = remote(ST.at[0], ST.at[1], s2s.at[0], s2r.at[0], Dzo)

time: 118 us -> 118 us (level)
  no operation moved by 1% of the time
where the time goes in v4:
time: 118 us; the launch traced here: 117 us
  Pallas kernels  115 us (97%)
  local copies, waits for them, and re-layouts  1.67 us (1%)
    pallas_call x1, Pallas kernels, on_device(): pl.pallas_call(kernel, out_shape=jax.ShapeDtypeStruct((SEQ, 256), BF16),...  115 us

profile of v4, /device:TPU:225, one launch (start us, length us, event | category | flops | bytes accessed | tf_op | source)
XLA Modules:
  0.0 117.1 jit_solution(9734623319238902676)
XLA Ops:
  0.0 115.4 %shard_map.73 = bf16[512,256]{1,0:T(8,128)(2,1)} custom-call(bf16[512,512]{1,0:T(8,128)(2,1)} %hid_in.1, bf16[512]{0:T(512)(128)(2,1)} %gain.1, bf16[16,4096]{1,0:T(8,128)(2,1)} %qw.1, bf16[16,512]{1,0:T(8,128)(2,1)} %kw.1, bf16[16,512]{1,0:T(8,128)(2,1)} %vw.1, f32[512,128]{1,0:T(8,128)} %constant.4.clone.cos_in, f32[512,128]{1,0:T(8,128)} %constant.5.clone.sin_in), custom_call_target="tpu_custom_call" | custom-call | tf_op jit(solution)/shard_map/pallas_call | solution.py:528
  115.4 1.7 %copy.9 = bf16[512,256]{1,0:T(8,128)(2,1)} copy(bf16[512,256]{1,0:T(8,128)(2,1)} %shard_map.73) | data formatting | bytes 524288
